TPU v7x, 32 devices: a whole 2x2x4 slice. The times are simulated.
32 devices in a mesh: dp: 4 (over x, core), ctx: 4 (over z), tensor: 2 (over y).
Axes of the slice: x: 2, y: 2, z: 4, core: 2. Of those that a mesh axis runs over, the one named last changes fastest.
Arguments:
- block_input: bfloat16 [12288, 2048], P(('dp', 'ctx'), 'tensor'), may hold values from -6 to 6
- cotangent: bfloat16 [12288, 2048], P(('dp', 'ctx'), 'tensor'), may hold values from -6 to 6
- deal_order: int32 [4, 4], P('dp'), may hold values from 0 to 3, as said below
- seq_lengths: int32 [12], P('dp'), may hold values from 96 to 2880, as said below
- seq_adapter: int32 [12], P('dp'), may hold values from 0 to 7
- mixer_gain: bfloat16 [2048], replicated, may hold values from 0.099609375 to 1.8984375
- ffn_gain: bfloat16 [2048], replicated, may hold values from 0.099609375 to 1.8984375
- conv_taps: bfloat16 [3, 2048], P(None, 'tensor'), may hold values from -3.5 to 3.5
- in_weight: bfloat16 [3, 2048, 2048], P(None, 'dp', 'tensor'), may hold values from -0.125 to 0.125
- out_weight: bfloat16 [2048, 2048], P('tensor', 'dp'), may hold values from -0.125 to 0.125
- gateup_weight: bfloat16 [2, 2048, 5632], P(None, 'dp', 'tensor'), may hold values from -0.125 to 0.125
- down_weight: bfloat16 [5632, 2048], P('tensor', 'dp'), may hold values from -0.078125 to 0.078125
- input_adapter_shrink: bfloat16 [2048, 128], replicated, may hold values from -0.125 to 0.125
- in_expand: bfloat16 [3, 128, 2048], P(None, None, 'tensor'), may hold values from -1.5 to 1.5
- out_shrink: bfloat16 [2048, 128], P('tensor'), may hold values from -0.125 to 0.125
- output_adapter_expand: bfloat16 [128, 2048], replicated, may hold values from -1.5 to 1.5
- ffn_shrink: bfloat16 [2048, 256], replicated, may hold values from -0.125 to 0.125
- ffn_expand: bfloat16 [2, 128, 5632], P(None, None, 'tensor'), may hold values from -1.5 to 1.5
- down_shrink: bfloat16 [5632, 128], P('tensor'), may hold values from -0.078125 to 0.078125
- down_adapter_expand: bfloat16 [128, 2048], replicated, may hold values from -1.5 to 1.5
Outputs:
- block_output: bfloat16 [12288, 2048], P(('dp', 'ctx'), 'tensor')
- input_grad: float32 [12288, 2048], P(('dp', 'ctx'), 'tensor')
- in_shrink_grad: float32 [2048, 128], replicated
- input_expand_gradient: float32 [3, 128, 2048], P(None, None, 'tensor')
- out_shrink_grad: float32 [2048, 128], P('tensor')
- output_expand_gradient: float32 [128, 2048], replicated
- ffn_shrink_grad: float32 [2048, 256], replicated
- feedforward_expand_gradient: float32 [2, 128, 5632], P(None, None, 'tensor')
- down_shrink_grad: float32 [5632, 128], P('tensor')
- down_adapter_expand_gradient: float32 [128, 2048], replicated
Inputs may be any that keep to these rules, and one draw needn't show every extreme that they name: `deal_order`: each row is a permutation of the 4 shard numbers. `seq_lengths`: each data group's 3 entries sum to 3072; all but one of them lie between 96 and 192.
All inputs are finite; a program needn't handle non-finite values.
Results may differ from a plain program's by a relative error of at most 0.013.
Values may be sent and summed in bfloat16 or wider, within the bound.
No kernel may reach another device: no remote copies, remote signals or barrier semaphores. Data moves between devices by JAX's collectives and lax.ppermute only.
A program may use at most 256 MiB of HBM per device.

v0:
```python
import jax
import jax.numpy as jnp
from jax import lax
from jax.sharding import PartitionSpec as P

RANK = 16
norm_eps = 1e-05
adapter_scale = 0.5


def shifted(block, axis, distance):
    devices = range(lax.axis_size(axis))
    route = [(i - distance, i) for i in devices if i - distance in devices]
    return lax.ppermute(block, axis, route)


def rms_scale(values):
    return lax.rsqrt(jnp.mean(values * values, axis=-1, keepdims=True) + norm_eps)


def norm_back(values, scale, gain, grad_out):
    unit = values * scale
    grad_unit = grad_out * gain
    return scale * (grad_unit - unit * jnp.mean(grad_unit * unit, axis=-1, keepdims=True))


def product_simple(left, right):
    return jnp.dot(left, right, preferred_element_type=jnp.float32)


def product_backward(left, right):
    return lax.dot_general(
        left, right, (((1,), (1,)), ((), ())), preferred_element_type=jnp.float32
    )


def product_leading(left, right):
    return lax.dot_general(
        left, right, (((0,), (0,)), ((), ())), preferred_element_type=jnp.float32
    )


def segment_of(positions, seq_ends):
    return jnp.sum((positions[:, None] >= seq_ends[None, :]).astype(jnp.int32), axis=1)


def fetch_mixer(in_weight, out_weight):
    return (
        lax.all_gather(in_weight, "dp", axis=1, tiled=True),
        lax.all_gather(out_weight, "dp", axis=1, tiled=True),
    )


def fetch_ffn(gateup_weight, down_weight):
    return (
        lax.all_gather(gateup_weight, "dp", axis=1, tiled=True),
        lax.all_gather(down_weight, "dp", axis=1, tiled=True),
    )


def body(
    block_input,
    cotangent,
    deal_order,
    seq_lengths,
    seq_adapter,
    mixer_gain,
    ffn_gain,
    conv_taps,
    in_weight,
    out_weight,
    gateup_weight,
    down_weight,
    input_adapter_shrink,
    in_expand,
    out_shrink,
    output_adapter_expand,
    ffn_shrink,
    ffn_expand,
    down_shrink,
    down_adapter_expand,
):
    tok_count = block_input.shape[0]
    half_width = block_input.shape[1]
    rank_cols = input_adapter_shrink.shape[1]
    part_index = lax.axis_index("tensor")
    group_total = lax.axis_size("dp")
    block_rows = tok_count // group_total
    deal_row = deal_order[0]
    slot_all = jnp.arange(group_total, dtype=jnp.int32)
    inverse_row = jnp.sum(
        jnp.where(deal_row[:, None] == slot_all[None, :], slot_all[:, None], 0), axis=0
    )
    dealt_in, dealt_cot = (
        lax.all_to_all(
            block_input.reshape(group_total, block_rows, half_width),
            "dp",
            split_axis=0,
            concat_axis=0,
            tiled=True,
        ),
        lax.all_to_all(
            cotangent.reshape(group_total, block_rows, half_width),
            "dp",
            split_axis=0,
            concat_axis=0,
            tiled=True,
        ),
    )
    packed_in = jnp.take(dealt_in, deal_row, axis=0).reshape(tok_count, half_width)
    packed_cot = jnp.take(dealt_cot, deal_row, axis=0).reshape(tok_count, half_width)
    seq_ends = jnp.cumsum(seq_lengths)[:-1]
    positions = lax.axis_index("ctx") * tok_count + jnp.arange(tok_count, dtype=jnp.int32)
    segment = segment_of(positions, seq_ends)
    slot_ids = jnp.arange(seq_lengths.shape[0], dtype=jnp.int32)
    token_adapter_index = jnp.sum(
        jnp.where(segment[:, None] == slot_ids[None, :], seq_adapter[None, :], 0), axis=1
    )
    column_group_index = jnp.arange(rank_cols, dtype=jnp.int32) // RANK
    adapter_mask = (column_group_index[None, :] == token_adapter_index[:, None]).astype(jnp.float32)
    adapter_half_float = adapter_mask.astype(jnp.bfloat16)
    adapter_mask_pair = jnp.concatenate([adapter_mask, adapter_mask], axis=1)
    pair_bf = adapter_mask_pair.astype(jnp.bfloat16)
    matching_first = ((positions >= 1) & (segment_of(positions - 1, seq_ends) == segment)).astype(
        jnp.float32
    )[:, None]
    matching_second = ((positions >= 2) & (segment_of(positions - 2, seq_ends) == segment)).astype(
        jnp.float32
    )[:, None]
    ahead_one = (segment_of(positions + 1, seq_ends) == segment).astype(jnp.float32)[:, None]
    ahead_two = (segment_of(positions + 2, seq_ends) == segment).astype(jnp.float32)[:, None]
    row_pair = (
        lax.all_gather(packed_in, "tensor", axis=1, tiled=True),
        lax.all_gather(packed_cot, "tensor", axis=1, tiled=True),
    )
    input_complete = row_pair[0].astype(jnp.float32)
    cotangent_half_float = row_pair[1]
    cot_full = cotangent_half_float.astype(jnp.float32)
    mixer_f = mixer_gain.astype(jnp.float32)
    ffn_f = ffn_gain.astype(jnp.float32)
    conv_w = conv_taps.astype(jnp.float32)
    in_full, out_full = fetch_mixer(in_weight, out_weight)
    scale_one = rms_scale(input_complete)
    normalized_rows = (input_complete * scale_one * mixer_f).astype(jnp.bfloat16)
    input_rank_rows = (
        product_simple(normalized_rows, input_adapter_shrink).astype(jnp.bfloat16)
        * adapter_half_float
    )
    projected_rows = jnp.einsum(
        "px,sxa->psa", normalized_rows, in_full, preferred_element_type=jnp.float32
    ) + adapter_scale * jnp.einsum(
        "fw,kwo->fko", input_rank_rows, in_expand, preferred_element_type=jnp.float32
    )
    gate_b = projected_rows[:, 0]
    gate_c = projected_rows[:, 1]
    values_x = projected_rows[:, 2]
    mixed = (gate_b * values_x).astype(jnp.bfloat16)
    prior = shifted(mixed[tok_count - 2 :], "ctx", 1)
    extended = jnp.concatenate([prior, mixed], axis=0).astype(jnp.float32)
    conv_out = (
        conv_w[0] * extended[2:]
        + conv_w[1] * extended[1:-1] * matching_first
        + conv_w[2] * extended[:-2] * matching_second
    )
    gated_rows = (gate_c * conv_out).astype(jnp.bfloat16)
    adapter_branch_sum, output_rank_sum = lax.psum(
        (product_simple(gated_rows, out_full), product_simple(gated_rows, out_shrink)), "tensor"
    )
    output_rank_rows = output_rank_sum.astype(jnp.bfloat16) * adapter_half_float
    hidden_state_rows = input_complete + (
        adapter_branch_sum + adapter_scale * product_simple(output_rank_rows, output_adapter_expand)
    )
    scale_two = rms_scale(hidden_state_rows)
    feedforward_input = (hidden_state_rows * scale_two * ffn_f).astype(jnp.bfloat16)
    feedforward_rank_rows = (
        product_simple(feedforward_input, ffn_shrink).astype(jnp.bfloat16) * pair_bf
    )
    ffn_low_split = feedforward_rank_rows.reshape(tok_count, 2, rank_cols)
    gu_full, down_full = fetch_ffn(gateup_weight, down_weight)
    gate_up_output = jnp.einsum(
        "cm,ame->cae", feedforward_input, gu_full, preferred_element_type=jnp.float32
    ) + adapter_scale * jnp.einsum(
        "vmc,mcb->vmb", ffn_low_split, ffn_expand, preferred_element_type=jnp.float32
    )
    gate_pre = gate_up_output[:, 0]
    up_pre = gate_up_output[:, 1]
    activated_rows = (jax.nn.silu(gate_pre) * up_pre).astype(jnp.bfloat16)
    down_weight_slice = lax.psum_scatter(
        product_simple(activated_rows, down_full).astype(jnp.bfloat16),
        "tensor",
        scatter_dimension=1,
        tiled=True,
    ).astype(jnp.float32)
    down_rank_rows_sum = lax.psum(product_simple(activated_rows, down_shrink), "tensor")
    down_rank_rows = down_rank_rows_sum.astype(jnp.bfloat16) * adapter_half_float
    expand_factor_slice = lax.dynamic_slice_in_dim(
        down_adapter_expand, part_index * half_width, half_width, 1
    )
    hidden_column_slice = lax.dynamic_slice_in_dim(
        hidden_state_rows, part_index * half_width, half_width, 1
    )
    packed_output = (
        hidden_column_slice
        + (down_weight_slice + adapter_scale * product_simple(down_rank_rows, expand_factor_slice))
    ).astype(jnp.bfloat16)
    gu_full, down_full = fetch_ffn(gateup_weight, down_weight)
    down_rank_gradient = (
        adapter_scale * product_backward(cotangent_half_float, down_adapter_expand) * adapter_mask
    ).astype(jnp.bfloat16)
    down_adapter_expand_gradient = adapter_scale * product_leading(
        down_rank_rows, cotangent_half_float
    )
    grad_act = product_backward(cotangent_half_float, down_full) + product_backward(
        down_rank_gradient, down_shrink
    )
    down_shrink_grad = product_leading(activated_rows, down_rank_gradient)
    sigmoid_gate = jax.nn.sigmoid(gate_pre)
    grad_gate = grad_act * up_pre * sigmoid_gate * (1.0 + gate_pre * (1.0 - sigmoid_gate))
    grad_up = grad_act * gate_pre * sigmoid_gate
    grad_gu = jnp.stack([grad_gate, grad_up], axis=1).astype(jnp.bfloat16)
    feedforward_expand_gradient = adapter_scale * jnp.einsum(
        "tje,tjf->jef", ffn_low_split, grad_gu, preferred_element_type=jnp.float32
    )
    feedforward_rank_part = adapter_scale * jnp.einsum(
        "tjf,jef->tje", grad_gu, ffn_expand, preferred_element_type=jnp.float32
    ).reshape(tok_count, 2 * rank_cols)
    ffn_in_part = jnp.einsum("tjf,jdf->td", grad_gu, gu_full, preferred_element_type=jnp.float32)
    ffn_in_sum, ffn_low_sum = lax.psum((ffn_in_part, feedforward_rank_part), "tensor")
    grad_ffn_low = (ffn_low_sum * adapter_mask_pair).astype(jnp.bfloat16)
    grad_ffn_in = ffn_in_sum + product_backward(grad_ffn_low, ffn_shrink)
    ffn_shrink_grad = product_leading(feedforward_input, grad_ffn_low)
    grad_hidden = cot_full + norm_back(hidden_state_rows, scale_two, ffn_f, grad_ffn_in)
    in_full, out_full = fetch_mixer(in_weight, out_weight)
    adapter_branch_gradient = grad_hidden.astype(jnp.bfloat16)
    out_rank_gradient = (
        adapter_scale
        * product_backward(adapter_branch_gradient, output_adapter_expand)
        * adapter_mask
    ).astype(jnp.bfloat16)
    output_expand_gradient = adapter_scale * product_leading(
        output_rank_rows, adapter_branch_gradient
    )
    grad_gated = product_backward(adapter_branch_gradient, out_full) + product_backward(
        out_rank_gradient, out_shrink
    )
    out_shrink_grad = product_leading(gated_rows, out_rank_gradient)
    grad_gate_c = grad_gated * conv_out
    grad_conv = grad_gated * gate_c
    ahead = shifted(grad_conv[:2], "ctx", -1)
    trailing = jnp.concatenate([grad_conv, ahead], axis=0)
    grad_mixed = (
        conv_w[0] * grad_conv
        + conv_w[1] * trailing[1:-1] * ahead_one
        + conv_w[2] * trailing[2:] * ahead_two
    )
    grad_proj = jnp.stack([grad_mixed * values_x, grad_gate_c, grad_mixed * gate_b], axis=1).astype(
        jnp.bfloat16
    )
    input_expand_gradient = adapter_scale * jnp.einsum(
        "te,tjc->jec", input_rank_rows, grad_proj, preferred_element_type=jnp.float32
    )
    input_rank_part = adapter_scale * jnp.einsum(
        "tjc,jec->te", grad_proj, in_expand, preferred_element_type=jnp.float32
    )
    normed_part = jnp.einsum("tjc,jdc->td", grad_proj, in_full, preferred_element_type=jnp.float32)
    normed_sum, input_rank_sum = lax.psum((normed_part, input_rank_part), "tensor")
    in_rank_gradient = (input_rank_sum * adapter_mask).astype(jnp.bfloat16)
    grad_normed = normed_sum + product_backward(in_rank_gradient, input_adapter_shrink)
    in_shrink_grad = product_leading(normalized_rows, in_rank_gradient)
    grad_input_full = grad_hidden + norm_back(input_complete, scale_one, mixer_f, grad_normed)
    packed_grad = lax.dynamic_slice_in_dim(grad_input_full, part_index * half_width, half_width, 1)
    output_blocks = jnp.take(
        packed_output.reshape(group_total, block_rows, half_width), inverse_row, axis=0
    )
    grad_blocks = jnp.take(
        packed_grad.reshape(group_total, block_rows, half_width), inverse_row, axis=0
    )
    block_output = lax.all_to_all(
        output_blocks, "dp", split_axis=0, concat_axis=0, tiled=True
    ).reshape(tok_count, half_width)
    input_grad = (
        lax.all_to_all(
            grad_blocks.astype(jnp.bfloat16), "dp", split_axis=0, concat_axis=0, tiled=True
        )
        .astype(grad_blocks.dtype)
        .reshape(tok_count, half_width)
    )
    totals = lax.psum(
        (
            in_shrink_grad,
            input_expand_gradient,
            out_shrink_grad,
            output_expand_gradient,
            ffn_shrink_grad,
            feedforward_expand_gradient,
            down_shrink_grad,
            down_adapter_expand_gradient,
        ),
        ("dp", "ctx"),
    )
    return (
        block_output,
        input_grad,
        totals[0],
        totals[1],
        totals[2],
        totals[3],
        totals[4],
        totals[5],
        totals[6],
        totals[7],
    )


def solution(mesh):
    placed = (
        P(("dp", "ctx"), "tensor"),
        P(("dp", "ctx"), "tensor"),
        P("dp", None),
        P("dp"),
        P("dp"),
        P(),
        P(),
        P(None, "tensor"),
        P(None, "dp", "tensor"),
        P("tensor", "dp"),
        P(None, "dp", "tensor"),
        P("tensor", "dp"),
        P(),
        P(None, None, "tensor"),
        P("tensor", None),
        P(),
        P(),
        P(None, None, "tensor"),
        P("tensor", None),
        P(),
    )
    return jax.shard_map(
        body,
        mesh=mesh,
        in_specs=placed,
        out_specs=(
            P(("dp", "ctx"), "tensor"),
            P(("dp", "ctx"), "tensor"),
            P(),
            P(None, None, "tensor"),
            P("tensor", None),
            P(),
            P(),
            P(None, None, "tensor"),
            P("tensor", None),
            P(),
        ),
        check_vma=False,
    )
```

profile of v0, /device:TPU:0, one launch (start us, length us, event | category | flops | bytes accessed | tf_op | source)
XLA Modules:
  0.0 1380.1 jit_solution(14482190222094816660)
XLA Ops:
  7.2 25.2 %all_to_all.20 = bf16[4,192,1024]{2,1,0:T(8,128)(2,1)} all-to-all(bf16[4,192,1024]{2,1,0:T(8,128)(2,1)} %bitcast.155), channel_id=1, replica_groups=mesh['dp'=4,'ctx'=4,'tensor'=2] {'dp'}, dimensions={0} | all-to-all | bytes 3145728 | tf_op jit(solution)/shard_map/all_to_all | solution.py:95
  39.3 16.7 %all-to-all-done.2 = bf16[4,192,1024]{2,1,0:T(8,128)(2,1)S(1)} async-done(((bf16[4,192,1024]{2,1,0:T(8,128)(2,1)}), bf16[4,192,1024]{2,1,0:T(8,128)(2,1)S(1)}, u32[]{:S(2)}, u32[]{:S(2)}) %all-to-all-start.2) | async-done | bytes 1572896 | tf_op jit(solution)/shard_map/all_to_all | solution.py:102
  65.6 42.4 %all-gather.7.cloned.1.call-done = bf16[768,2048]{1,0:T(8,128)(2,1)} async-done(((bf16[768,1024]{1,0:T(8,128)(2,1)}), bf16[768,2048]{1,0:T(8,128)(2,1)}) %all-gather.7.cloned.1.call-update) | async-done | bytes 3145744 | tf_op jit(solution)/shard_map/all_gather | solution.py:133
  111.9 79.8 %all-gather.9.cloned.1.call-done = bf16[3,2048,1024]{2,1,0:T(8,128)(2,1)} async-done(((bf16[3,512,1024]{2,1,0:T(8,128)(2,1)}), bf16[3,2048,1024]{2,1,0:T(8,128)(2,1)}) %all-gather.9.cloned.1.call-update) | async-done | bytes 12582928 | tf_op jit(solution)/shard_map/all_gather | solution.py:49
  191.7 13.6 fusion.17
  215.4 12.4 all-gather.11.cloned.1.call-done
  227.8 7.4 fusion.72
  237.9 36.9 %all-gather.17.cloned.1.call-done = bf16[768,2048]{1,0:T(8,128)(2,1)} async-done(((bf16[768,1024]{1,0:T(8,128)(2,1)}), bf16[768,2048]{1,0:T(8,128)(2,1)}) %all-gather.17.cloned.1.call-update) | async-done | bytes 3145744 | tf_op jit(solution)/shard_map/all_gather | solution.py:134
  278.3 74.0 %all-gather.15.cloned.1.call-done = bf16[2816,2048]{1,0:T(8,128)(2,1)} async-done(((bf16[2816,512]{1,0:T(8,128)(2,1)}), bf16[2816,2048]{1,0:T(8,128)(2,1)}) %all-gather.15.cloned.1.call-update) | async-done | bytes 11534352 | tf_op jit(solution)/shard_map/all_gather | solution.py:57
  352.3 15.8 %fusion.75 = f32[768,2816]{1,0:T(8,128)} fusion(bf16[768,2048]{1,0:T(8,128)(2,1)} %all-gather.17.cloned.1.call-done, bf16[2816,2048]{1,0:T(8,128)(2,1)} %all-gather.15.cloned.1.call-done), kind=kOutput, calls=%fused_computation.166 | convolution fusion | flops 8858370048 | bytes 23330816 | tf_op jit(solution)/shard_map/dot_general | solution.py:32
  369.5 25.5 %all-reduce.17 = bf16[768,128]{1,0:T(8,128)(2,1)S(1)} all-reduce(f32[768,128]{1,0:T(8,128)} %fusion.73), channel_id=1, replica_groups=mesh['dp'=4,'ctx'=4,'tensor'=2] {'tensor'}, use_global_device_ids=true, to_apply=%region_7.9 | all-reduce | flops 98304 | bytes 589824 | tf_op jit(solution)/shard_map/psum | solution.py:166
  395.0 121.3 %all-reduce.10.cloned.1.call-done = f32[768,2048]{1,0:T(8,128)} async-done(((f32[768,2048]{1,0:T(8,128)}), f32[768,2048]{1,0:T(8,128)}) %all-reduce.10.cloned.1.call-update) | async-done | bytes 6291472 | tf_op jit(solution)/shard_map/psum | solution.py:166
  528.2 131.7 %all-gather.13.cloned.1.call-done = bf16[2,2048,2816]{2,1,0:T(8,128)(2,1)} async-done(((bf16[2,512,2816]{2,1,0:T(8,128)(2,1)}), bf16[2,2048,2816]{2,1,0:T(8,128)(2,1)}) %all-gather.13.cloned.1.call-update) | async-done | bytes 23068688 | tf_op jit(solution)/shard_map/all_gather | solution.py:56
  659.9 23.8 %fusion.15 = f32[768,2,2816]{2,0,1:T(8,128)S(1)} fusion(bf16[2,2048,2816]{2,1,0:T(8,128)(2,1)} %all-gather.13.cloned.1.call-done, bf16[768,2048]{1,0:T(8,128)(2,1)} %copy-done.11), kind=kOutput, calls=%fused_computation.57 | convolution fusion | flops 17716740096 | bytes 43515904 | tf_op jit(solution)/shard_map/cm,ame->cae/dot_general | solution.py:180
  683.6 9.4 bitcast_add_fusion
  693.0 13.5 fusion.2
  713.6 25.4 %convolution_bitcast_fusion.1 = f32[768,2048]{1,0:T(8,128)} fusion(bf16[2,2048,2816]{2,1,0:T(8,128)(2,1)} %all-gather.13.cloned.1.call-done, bf16[768,1,2816]{2,0,1:T(8,128)(2,1)} %get-tuple-element.53, bf16[768,1,2816]{2,0,1:T(8,128)(2,1)} %copy-done.65), kind=kOutput, calls=%fused_computation.31 | convolution fusion | flops 17721065472 | bytes 38010880 | tf_op jit(solution)/shard_map/tjf,jdf->td/dot_general | solution.py:227
  739.0 14.4 %convolution_convert_fusion = bf16[768,2048]{1,0:T(8,128)(2,1)} fusion(bf16[768,2816]{1,0:T(8,128)(2,1)} %get-tuple-element.54, bf16[2816,2048]{1,0:T(8,128)(2,1)} %all-gather.15.cloned.1.call-done), kind=kOutput, calls=%fused_computation.32 | convolution fusion | flops 8859942912 | bytes 19005440 | tf_op jit(solution)/shard_map/dot_general | solution.py:28
  753.6 156.1 %all-reduce.16.cloned.1.call-done = (f32[768,2048]{1,0:T(8,128)}, f32[768,256]{1,0:T(8,128)}) async-done(((f32[768,2048]{1,0:T(8,128)}, f32[768,256]{1,0:T(8,128)}), (f32[768,2048]{1,0:T(8,128)}, f32[768,256]{1,0:T(8,128)})) %all-reduce.16.cloned.1.call-update) | async-done | bytes 7077904 | tf_op jit(solution)/shard_map/psum | solution.py:228
  940.3 14.7 %convolution_bitcast_fusion = f32[768,2048]{1,0:T(8,128)} fusion(bf16[3,2048,1024]{2,1,0:T(8,128)(2,1)} %all-gather.9.cloned.1.call-done, bf16[768,1,1024]{2,0,1:T(8,128)(2,1)S(1)} %fusion.23, bf16[768,1,1024]{2,0,1:T(8,128)(2,1)S(1)} %get-tuple-element.57, bf16[768,1,1024]{2,0,1:T(8,128)(2,1)S(1)} %get-tuple-element.48), kind=kOutput, calls=%fused_computation.30 | convolution fusion | flops 9668395008 | bytes 23592960 | tf_op jit(solution)/shard_map/tjc,jdc->td/dot_general | solution.py:265
  978.8 41.3 %all-reduce.18 = (bf16[768,128]{1,0:T(8,128)(2,1)S(1)}, bf16[768,128]{1,0:T(8,128)(2,1)S(1)}) all-reduce(f32[768,128]{1,0:T(8,128)S(1)} %fusion.74, f32[768,128]{1,0:T(8,128)S(1)} %fusion.27), channel_id=1, replica_groups=mesh['dp'=4,'ctx'=4,'tensor'=2] {'tensor'}, use_global_device_ids=true, to_apply=%region_10.12 | all-reduce | flops 196608 | bytes 1179648 | tf_op jit(solution)/shard_map/psum | solution.py:194
  1035.0 92.8 %all-reduce.12.cloned.1.call-done = f32[768,2048]{1,0:T(8,128)} async-done(((f32[768,2048]{1,0:T(8,128)}), f32[768,2048]{1,0:T(8,128)}) %all-reduce.12.cloned.1.call-update) | async-done | bytes 6291472 | tf_op jit(solution)/shard_map/psum | solution.py:266
  1141.1 39.8 %all_to_all.21 = bf16[4,192,1024]{2,1,0:T(8,128)(2,1)S(1)} all-to-all(bf16[4,192,1024]{2,1,0:T(8,128)(2,1)S(1)} %get-tuple-element.67), channel_id=1, replica_groups=mesh['dp'=4,'ctx'=4,'tensor'=2] {'dp'}, dimensions={0} | all-to-all | bytes 3145728 | tf_op jit(solution)/shard_map/all_to_all | solution.py:278
  1185.3 170.9 %all-reduce.14.cloned.1.call-done = (f32[2048,128]{1,0:T(8,128)}, f32[3,128,1024]{1,2,0:T(8,128)}, f32[1024,128]{1,0:T(8,128)}, f32[128,2048]{1,0:T(8,128)}, f32...) async-done(((f32[2048,128]{1,0:T(8,128)}, f32[3,128,1024]{1,2,0:T(8,128)}, f32[1024,128]{1,0:T(8,128)}, ...) | async-done | bytes 11665424 | tf_op jit(solution)/shard_map/psum | solution.py:288
  (258 shorter events, 159.8 us)
Async XLA Ops:
  7.2 676.5 %copy-start = (bf16[2,128,2816]{2,1,0:T(8,128)(2,1)S(1)}, bf16[2,128,2816]{2,1,0:T(8,128)(2,1)}, u32[]{:S(2)}) copy-start(bf16[2,128,2816]{2,1,0:T(8,128)(2,1)} %param.39) | copy-start | bytes 4325380
  32.4 23.6 %all-to-all-start.2 = ((bf16[4,192,1024]{2,1,0:T(8,128)(2,1)}), bf16[4,192,1024]{2,1,0:T(8,128)(2,1)S(1)}, u32[]{:S(2)}, u32[]{:S(2)}) async-start(bf16[4,192,1024]{2,1,0:T(8,128)(2,1)} %bitcast.156), calls=%async_computation.3 | async-start | bytes 3145728 | tf_op jit(solution)/shard_map/all_to_all | solution.py:102
  36.0 72.0 %all-gather.7.cloned.1.call-start = ((), (), s32[]{:S(2)}) async-start(), calls=%async_computation.5 | async-start | bytes 4718592 | tf_op jit(solution)/shard_map/all_gather | solution.py:133
  61.8 130.0 %all-gather.9.cloned.1.call-start = ((), (), s32[]{:S(2)}) async-start(), calls=%async_computation.6 | async-start | bytes 15728640 | tf_op jit(solution)/shard_map/all_gather | solution.py:49
  62.6 165.3 %all-gather.11.cloned.1.call-start = ((), (), s32[]{:S(2)}) async-start(), calls=%async_computation.7 | async-start | bytes 5242880 | tf_op jit(solution)/shard_map/all_gather | solution.py:50
  63.3 211.5 %all-gather.17.cloned.1.call-start = ((), (), s32[]{:S(2)}) async-start(), calls=%async_computation.12 | async-start | bytes 4718592 | tf_op jit(solution)/shard_map/all_gather | solution.py:134
  63.9 288.5 %all-gather.15.cloned.1.call-start = ((), (), s32[]{:S(2)}) async-start(), calls=%async_computation.10 | async-start | bytes 14417920 | tf_op jit(solution)/shard_map/all_gather | solution.py:57
  64.5 451.9 %all-reduce.10.cloned.1.call-start = ((), (), s32[]{:S(2)}) async-start(), calls=%async_computation.8 | async-start | bytes 12582912 | tf_op jit(solution)/shard_map/psum | solution.py:166
  64.5 127.2 %copy-start.54 = (f32[2048]{0:T(1024)}, f32[2048]{0:T(1024)S(1)}, u32[]{:S(2)}) copy-start(f32[2048]{0:T(1024)S(1)} %convert_element_type.128) | copy-start | bytes 24580
  111.9 93.4 %copy-start.41 = (bf16[768,128,1]{1,0,2:T(8,128)(2,1)}, bf16[768,128,1]{1,0,2:T(8,128)(2,1)S(1)}, u32[]{:S(2)}) copy-start(bf16[768,128,1]{1,0,2:T(8,128)(2,1)S(1)} %fusion.32) | copy-start | bytes 589828
  207.3 4.7 collective-permute-start
  215.4 152.8 %copy-start.7 = (bf16[768,1024]{1,0:T(8,128)(2,1)}, bf16[768,1024]{1,0:T(8,128)(2,1)S(1)}, u32[]{:S(2)}) copy-start(bf16[768,1024]{1,0:T(8,128)(2,1)S(1)} %get-tuple-element.50) | copy-start | bytes 4718596
  235.2 424.6 %all-gather.13.cloned.1.call-start = ((), (), s32[]{:S(2)}) async-start(), calls=%async_computation.9 | async-start | bytes 28835840 | tf_op jit(solution)/shard_map/all_gather | solution.py:56
  236.0 673.7 %all-reduce.16.cloned.1.call-start = ((), (), s32[]{:S(2)}) async-start(), calls=%async_computation.15 | async-start | bytes 14155776 | tf_op jit(solution)/shard_map/psum | solution.py:228
  368.2 148.1 %copy-start.14 = (bf16[128,2048]{1,0:T(8,128)(2,1)S(1)}, bf16[128,2048]{1,0:T(8,128)(2,1)}, u32[]{:S(2)}) copy-start(bf16[128,2048]{1,0:T(8,128)(2,1)} %param.37) | copy-start | bytes 1572868
  395.0 126.0 %copy-start.16 = (bf16[768,128]{1,0:T(8,128)(2,1)}, bf16[768,128]{1,0:T(8,128)(2,1)S(1)}, u32[]{:S(2)}) copy-start(bf16[768,128]{1,0:T(8,128)(2,1)S(1)} %all-reduce.17) | copy-start | bytes 589828
  739.0 290.9 %reduce-scatter.2.cloned.1.call-start = ((), (), s32[]{:S(2)}) async-start(), calls=%async_computation.11 | async-start | bytes 4718592 | tf_op jit(solution)/shard_map/reduce_scatter | solution.py:188
  753.5 156.2 %copy-start.26 = (f32[768,128]{1,0:T(8,128)S(1)}, f32[768,128]{1,0:T(8,128)}, u32[]{:S(2)}) copy-start(f32[768,128]{1,0:T(8,128)} %compare_convert_fusion) | copy-start | bytes 1179652
  753.5 156.2 %copy-start.31 = (bf16[2048,256]{1,0:T(8,128)(2,1)S(1)}, bf16[2048,256]{1,0:T(8,128)(2,1)}, u32[]{:S(2)}) copy-start(bf16[2048,256]{1,0:T(8,128)(2,1)} %param.38) | copy-start | bytes 3145732
  753.5 374.3 %all-reduce.12.cloned.1.call-start = ((), (), s32[]{:S(2)}) async-start(), calls=%async_computation.13 | async-start | bytes 12582912 | tf_op jit(solution)/shard_map/psum | solution.py:266
  929.3 5.5 collective-permute-start.1
  955.0 401.1 %all-reduce.14.cloned.1.call-start = ((), (), s32[]{:S(2)}) async-start(), calls=%async_computation.14 | async-start | bytes 23330816 | tf_op jit(solution)/shard_map/psum | solution.py:288
  1033.2 94.6 %copy-start.39 = (bf16[2048,128]{1,0:T(8,128)(2,1)S(1)}, bf16[2048,128]{1,0:T(8,128)(2,1)}, u32[]{:S(2)}) copy-start(bf16[2048,128]{1,0:T(8,128)(2,1)} %param.34) | copy-start | bytes 1572868
  1180.9 178.3 %all-to-all-start.3 = ((bf16[4,192,1024]{2,1,0:T(8,128)(2,1)}), bf16[4,192,1024]{2,1,0:T(8,128)(2,1)}, u32[]{:S(2)}, u32[]{:S(2)}) async-start(bf16[4,192,1024]{2,1,0:T(8,128)(2,1)} %get-tuple-element.66), calls=%async_computation.4 | async-start | bytes 3145728 | tf_op jit(solution)/shard_map/all_to_all | solution.py:282
  (64 other events, 636.3 us)
Sparse Core Ops, SparseCore 0:
  61.9 46.0 all-gather.6
  109.6 82.0 all-gather.8
  193.3 34.4 all-gather.10
  229.8 44.9 all-gather.16
  276.2 76.1 all-gather.14
  354.6 161.6 all-reduce.9
  518.0 141.8 all-gather.12
  739.1 170.5 all-reduce.15
  911.9 43.3 reduce-scatter.1
  957.7 170.0 all-reduce.11
  1133.8 222.3 all-reduce.13
where the time goes:
time: 1390 us; the launch traced here: 1380 us
  waiting for transfers between devices  944 us (68%)
  matrix products  208 us (15%)
  blocking collectives  132 us (9%)
  local copies, waits for them, and re-layouts  36.4 us (3%)
  other arithmetic  31.6 us (2%)
  between operations  15.3 us (1%)
    psum x1, waiting for transfers between devices, body(): lax.psum((in_shrink_grad, input_expand_gradient, out_shrink_grad, output_...  171 us
    psum x1, waiting for transfers between devices, body(): lax.psum((ffn_in_part, feedforward_rank_part), 'tensor')  156 us
    all_gather x1, waiting for transfers between devices, fetch_ffn(): lax.all_gather(gateup_weight, 'dp', axis=1, tiled=True)  132 us
    psum x1, waiting for transfers between devices, body(): lax.psum((product_simple(gated_rows, out_full), product_simple(gated_rows...  121 us
    psum x1, waiting for transfers between devices, body(): lax.psum((normed_part, input_rank_part), 'tensor')  92.8 us
    all_gather x1, waiting for transfers between devices, fetch_mixer(): lax.all_gather(in_weight, 'dp', axis=1, tiled=True)  79.8 us
    all_gather x1, waiting for transfers between devices, fetch_ffn(): lax.all_gather(down_weight, 'dp', axis=1, tiled=True)  74 us
    dot_general x8, matrix products, product_backward(): lax.dot_general(left, right, (((1,), (1,)), ((), ())), preferred_element_...  49.3 us
  transfers between devices with their start and end apart: 15, of which 13 were waited for; matrix products, arithmetic and copies ran while one was open for 12% of the time, Pallas kernels for 0%

commit v1 on v0

--- a/solution.py
+++ b/solution.py
@@ -8,6 +8,19 @@
 adapter_scale = 0.5
 
 
+def ring_gather(array, axis, dim):
+    size, mine, extent = (lax.axis_size(axis), lax.axis_index(axis), array.shape[dim])
+    ahead = [(i, (i + 1) % size) for i in range(size)]
+    result = jnp.zeros((*array.shape[:dim], size * extent, *array.shape[dim + 1 :]), array.dtype)
+    current = array
+    for lap in range(size):
+        owner = (mine - lap) % size
+        result = lax.dynamic_update_slice_in_dim(result, current, owner * extent, axis=dim)
+        if lap < size - 1:
+            current = lax.ppermute(current, axis, ahead)
+    return result
+
+
 def shifted(block, axis, distance):
     devices = range(lax.axis_size(axis))
     route = [(i - distance, i) for i in devices if i - distance in devices]
@@ -53,7 +66,7 @@
 
 def fetch_ffn(gateup_weight, down_weight):
     return (
-        lax.all_gather(gateup_weight, "dp", axis=1, tiled=True),
+        ring_gather(gateup_weight, "dp", 1),
         lax.all_gather(down_weight, "dp", axis=1, tiled=True),
     )
 

time: 1390 us -> 1320 us (0.950)
  waiting for transfers between devices: 944 us -> 827 us
  local copies, waits for them, and re-layouts: 36.4 us -> 70.6 us
    ppermute x0 -> x3, waiting for transfers between devices: none -> 235 us  [ring_gather(): current = lax.ppermute(current, axis, ahead)]
    all_gather x1 -> x0, waiting for transfers between devices: 132 us -> none  [fetch_ffn(): lax.all_gather(gateup_weight, 'dp', axis=1, tiled=True)]
    all_gather x1, waiting for transfers between devices: 79.8 us -> 0.01 us  [fetch_mixer(): lax.all_gather(in_weight, 'dp', axis=1, tiled=True)]
    all_gather x1, waiting for transfers between devices: 74 us -> 29.7 us  [fetch_ffn(): lax.all_gather(down_weight, 'dp', axis=1, tiled=True)]
    all_gather x1, waiting for transfers between devices: 42.4 us -> 0.01 us  [body(): lax.all_gather(packed_in, 'tensor', axis=1, tiled=True)]
    all_gather x1, waiting for transfers between devices: 36.9 us -> 0.01 us  [body(): lax.all_gather(packed_cot, 'tensor', axis=1, tiled=True)]
    dynamic_update_slice x0 -> x4, local copies, waits for them, and re-layouts: none -> 23.2 us  [ring_gather(): lax.dynamic_update_slice_in_dim(result, current, owner * extent, axis=dim)]
    unnamed x155 -> x183, local copies, waits for them, and re-layouts: 25.7 us -> 29.1 us
  transfers between devices with their start and end apart: 15 -> 17, of which waited for: 13 -> 11; matrix products, arithmetic and copies ran while one was open for 12% -> 15% of each run, Pallas kernels for 0% -> 0%
where the time goes in v1:
time: 1320 us; the launch traced here: 1310 us
  waiting for transfers between devices  827 us (63%)
  matrix products  219 us (17%)
  blocking collectives  132 us (10%)
  local copies, waits for them, and re-layouts  70.6 us (5%)
  other arithmetic  34.7 us (3%)
  between operations  15.9 us (1%)
  starting transfers between devices  14.5 us (1%)
    ppermute x3, waiting for transfers between devices, ring_gather(): current = lax.ppermute(current, axis, ahead)  235 us
    psum x1, waiting for transfers between devices, body(): lax.psum((in_shrink_grad, input_expand_gradient, out_shrink_grad, output_...  171 us
    psum x1, waiting for transfers between devices, body(): lax.psum((ffn_in_part, feedforward_rank_part), 'tensor')  156 us
    psum x1, waiting for transfers between devices, body(): lax.psum((product_simple(gated_rows, out_full), product_simple(gated_rows...  121 us
    psum x1, waiting for transfers between devices, body(): lax.psum((normed_part, input_rank_part), 'tensor')  89.9 us
    dot_general x8, matrix products, product_backward(): lax.dot_general(left, right, (((1,), (1,)), ((), ())), preferred_element_...  55.9 us
    psum x1, blocking collectives, body(): lax.psum(product_simple(activated_rows, down_shrink), 'tensor')  40.4 us
    all_to_all x1, blocking collectives, body(): lax.all_to_all(output_blocks, 'dp', split_axis=0, concat_axis=0, tiled=True)  39.8 us
  transfers between devices with their start and end apart: 17, of which 11 were waited for; matrix products, arithmetic and copies ran while one was open for 15% of the time, Pallas kernels for 0%

profile of v1, /device:TPU:0, one launch (start us, length us, event | category | flops | bytes accessed | tf_op | source)
XLA Modules:
  0.0 1313.2 jit_solution(13714668586375870277)
XLA Ops:
  7.2 25.3 %all_to_all.20 = bf16[4,192,1024]{2,1,0:T(8,128)(2,1)} all-to-all(bf16[4,192,1024]{2,1,0:T(8,128)(2,1)} %bitcast.155), channel_id=1, replica_groups=mesh['dp'=4,'ctx'=4,'tensor'=2] {'dp'}, dimensions={0} | all-to-all | bytes 3145728 | tf_op jit(solution)/shard_map/all_to_all | solution.py:108
  39.3 16.8 %all-to-all-done.2 = bf16[4,192,1024]{2,1,0:T(8,128)(2,1)S(1)} async-done(((bf16[4,192,1024]{2,1,0:T(8,128)(2,1)}), bf16[4,192,1024]{2,1,0:T(8,128)(2,1)S(1)}, u32[]{:S(2)}, u32[]{:S(2)}) %all-to-all-start.2) | async-done | bytes 1572896 | tf_op jit(solution)/shard_map/all_to_all | solution.py:115
  64.6 79.4 %collective-permute-done.1 = bf16[2,512,2816]{2,1,0:T(8,128)(2,1)} collective-permute-done((bf16[2,512,2816]{2,1,0:T(8,128)(2,1)}, bf16[2,512,2816]{2,1,0:T(8,128)(2,1)}, u32[]{:S(2)}, u32[]{:S(2)}) %collective-permute-start.1) | collective-permute-done | bytes 5767200 | tf_op jit(solution)/shard_map/ppermute | solution.py:20
  151.6 129.7 %collective-permute-done.2 = bf16[2,512,2816]{2,1,0:T(8,128)(2,1)} collective-permute-done((bf16[2,512,2816]{2,1,0:T(8,128)(2,1)}, bf16[2,512,2816]{2,1,0:T(8,128)(2,1)}, u32[]{:S(2)}, u32[]{:S(2)}) %collective-permute-start.2) | collective-permute-done | bytes 5767200 | tf_op jit(solution)/shard_map/ppermute | solution.py:20
  281.4 14.2 %fusion.16 = f32[768,3,1024]{2,0,1:T(8,128)S(1)} fusion(bf16[3,2048,1024]{2,1,0:T(8,128)(2,1)} %all-gather.8.cloned.1.call-done, f32[2048]{0:T(1024)S(1)} %convert_element_type.128, f32[768]{0:T(1024)S(1)} %add_rsqrt_fusion.1, bf16[768,2048]{1,0:T(8,128)(2,1)} %all-gather.6.cloned.1.call-done), kind=kOutput, calls=%fused_computation.58 | convolution fusion | flops 9669967872 | bytes 25177088 | tf_op jit(solution)/shard_map/px,sxa->psa/dot_general | solution.py:162
  311.3 8.0 fusion.72
  319.6 8.5 broadcast.215
  349.4 25.6 %collective-permute-done.3 = bf16[2,512,2816]{2,1,0:T(8,128)(2,1)} collective-permute-done((bf16[2,512,2816]{2,1,0:T(8,128)(2,1)}, bf16[2,512,2816]{2,1,0:T(8,128)(2,1)}, u32[]{:S(2)}, u32[]{:S(2)}) %collective-permute-start.3) | collective-permute-done | bytes 5767200 | tf_op jit(solution)/shard_map/ppermute | solution.py:20
  380.4 29.7 %all-gather.12.cloned.1.call-done = bf16[2816,2048]{1,0:T(8,128)(2,1)} async-done(((bf16[2816,512]{1,0:T(8,128)(2,1)}), bf16[2816,2048]{1,0:T(8,128)(2,1)}) %all-gather.12.cloned.1.call-update) | async-done | bytes 11534352 | tf_op jit(solution)/shard_map/all_gather | solution.py:70
  410.1 15.9 %fusion.76 = f32[768,2816]{1,0:T(8,128)} fusion(bf16[768,2048]{1,0:T(8,128)(2,1)} %all-gather.14.cloned.1.call-done, bf16[2816,2048]{1,0:T(8,128)(2,1)} %all-gather.12.cloned.1.call-done), kind=kOutput, calls=%fused_computation.171 | convolution fusion | flops 8858370048 | bytes 23330816 | tf_op jit(solution)/shard_map/dot_general | solution.py:45
  427.3 26.8 %all-reduce.17 = bf16[768,128]{1,0:T(8,128)(2,1)S(1)} all-reduce(f32[768,128]{1,0:T(8,128)} %fusion.73), channel_id=1, replica_groups=mesh['dp'=4,'ctx'=4,'tensor'=2] {'tensor'}, use_global_device_ids=true, to_apply=%region_7.9 | all-reduce | flops 98304 | bytes 589824 | tf_op jit(solution)/shard_map/psum | solution.py:179
  454.1 121.1 %all-reduce.10.cloned.1.call-done = f32[768,2048]{1,0:T(8,128)} async-done(((f32[768,2048]{1,0:T(8,128)}), f32[768,2048]{1,0:T(8,128)}) %all-reduce.10.cloned.1.call-update) | async-done | bytes 6291472 | tf_op jit(solution)/shard_map/psum | solution.py:179
  585.4 8.3 fusion.74
  593.8 26.8 %bitcast_add_fusion = f32[768,2,2816]{2,0,1:T(8,128)} fusion(f32[2,768,2816]{2,1,0:T(8,128)} %fusion.74, bf16[2,2048,2816]{2,1,0:T(8,128)(2,1)} %constant_dynamic-update-slice_fusion, bf16[768,2048]{1,0:T(8,128)(2,1)S(1)} %copy-done.11), kind=kOutput, calls=%fused_computation.4 | convolution fusion | flops 17725390848 | bytes 60817408 | tf_op jit(solution)/shard_map/cm,ame->cae/dot_general | solution.py:193
  620.6 14.5 %fusion.2 = (bf16[768,1,2816]{2,0,1:T(8,128)(2,1)S(1)}, bf16[768,1,2816]{2,0,1:T(8,128)(2,1)}, bf16[768,2816]{1,0:T(8,128)(2,1)}) fusion(f32[768,2,2816]{2,0,1:T(8,128)} %bitcast_add_fusion, f32[768,2816]{1,0:T(8,128)} %fusion.76, bf16[768,128]{1,0:T(8,128)(2,1)S(1)} %copy-done.48, bf16[2816,128]{1,0:T(8,128)(2,1)S(1)} %copy-done.40), kind=kOutput, calls=%fused_computation.28 | convolution fusion | flops 590413824 | bytes 39845888 | tf_op jit(solution)/shard_map/dot_general | solution.py:45
  640.9 24.0 %convolution_bitcast_fusion.1 = f32[768,2048]{1,0:T(8,128)} fusion(bf16[2,2048,2816]{2,1,0:T(8,128)(2,1)} %constant_dynamic-update-slice_fusion, bf16[768,1,2816]{2,0,1:T(8,128)(2,1)} %get-tuple-element.53, bf16[768,1,2816]{2,0,1:T(8,128)(2,1)S(1)} %get-tuple-element.52), kind=kOutput, calls=%fused_computation.31 | convolution fusion | flops 17721065472 | bytes 38010880 | tf_op jit(solution)/shard_map/tjf,jdf->td/dot_general | solution.py:240
  666.1 14.4 %convolution_convert_fusion = bf16[768,2048]{1,0:T(8,128)(2,1)} fusion(bf16[768,2816]{1,0:T(8,128)(2,1)} %get-tuple-element.54, bf16[2816,2048]{1,0:T(8,128)(2,1)} %all-gather.12.cloned.1.call-done), kind=kOutput, calls=%fused_computation.32 | convolution fusion | flops 8859942912 | bytes 19005440 | tf_op jit(solution)/shard_map/dot_general | solution.py:41
  680.6 156.1 %all-reduce.16.cloned.1.call-done = (f32[768,2048]{1,0:T(8,128)}, f32[768,256]{1,0:T(8,128)}) async-done(((f32[768,2048]{1,0:T(8,128)}, f32[768,256]{1,0:T(8,128)}), (f32[768,2048]{1,0:T(8,128)}, f32[768,256]{1,0:T(8,128)})) %all-reduce.16.cloned.1.call-update) | async-done | bytes 7077904 | tf_op jit(solution)/shard_map/psum | solution.py:241
  836.8 9.6 multiply_reduce_fusion.1
  876.6 14.7 %convolution_bitcast_fusion = f32[768,2048]{1,0:T(8,128)} fusion(bf16[3,2048,1024]{2,1,0:T(8,128)(2,1)} %all-gather.8.cloned.1.call-done, bf16[768,1,1024]{2,0,1:T(8,128)(2,1)S(1)} %fusion.22, bf16[768,1,1024]{2,0,1:T(8,128)(2,1)S(1)} %get-tuple-element.57, bf16[768,1,1024]{2,0,1:T(8,128)(2,1)S(1)} %get-tuple-element.48), kind=kOutput, calls=%fused_computation.30 | convolution fusion | flops 9668395008 | bytes 23592960 | tf_op jit(solution)/shard_map/tjc,jdc->td/dot_general | solution.py:278
  915.7 40.4 %all-reduce.18 = (bf16[768,128]{1,0:T(8,128)(2,1)S(1)}, bf16[768,128]{1,0:T(8,128)(2,1)S(1)}) all-reduce(f32[768,128]{1,0:T(8,128)S(1)} %fusion.75, f32[768,128]{1,0:T(8,128)S(1)} %fusion.26), channel_id=1, replica_groups=mesh['dp'=4,'ctx'=4,'tensor'=2] {'tensor'}, use_global_device_ids=true, to_apply=%region_10.12 | all-reduce | flops 196608 | bytes 1179648 | tf_op jit(solution)/shard_map/psum | solution.py:207
  971.1 89.9 %all-reduce.12.cloned.1.call-done = f32[768,2048]{1,0:T(8,128)} async-done(((f32[768,2048]{1,0:T(8,128)}), f32[768,2048]{1,0:T(8,128)}) %all-reduce.12.cloned.1.call-update) | async-done | bytes 6291472 | tf_op jit(solution)/shard_map/psum | solution.py:279
  1074.3 39.8 %all_to_all.21 = bf16[4,192,1024]{2,1,0:T(8,128)(2,1)S(1)} all-to-all(bf16[4,192,1024]{2,1,0:T(8,128)(2,1)S(1)} %get-tuple-element.67), channel_id=1, replica_groups=mesh['dp'=4,'ctx'=4,'tensor'=2] {'dp'}, dimensions={0} | all-to-all | bytes 3145728 | tf_op jit(solution)/shard_map/all_to_all | solution.py:291
  1118.4 170.5 %all-reduce.14.cloned.1.call-done = (f32[2048,128]{1,0:T(8,128)}, f32[3,128,1024]{1,2,0:T(8,128)}, f32[1024,128]{1,0:T(8,128)}, f32[128,2048]{1,0:T(8,128)}, f32...) async-done(((f32[2048,128]{1,0:T(8,128)}, f32[3,128,1024]{1,2,0:T(8,128)}, f32[1024,128]{1,0:T(8,128)}, ...) | async-done | bytes 11665424 | tf_op jit(solution)/shard_map/psum | solution.py:301
  (295 shorter events, 187.5 us)
Async XLA Ops:
  7.2 578.3 %copy-start = (bf16[2,128,2816]{2,1,0:T(8,128)(2,1)S(1)}, bf16[2,128,2816]{2,1,0:T(8,128)(2,1)}, u32[]{:S(2)}) copy-start(bf16[2,128,2816]{2,1,0:T(8,128)(2,1)} %param.39) | copy-start | bytes 4325380
  32.5 23.6 %all-to-all-start.2 = ((bf16[4,192,1024]{2,1,0:T(8,128)(2,1)}), bf16[4,192,1024]{2,1,0:T(8,128)(2,1)S(1)}, u32[]{:S(2)}, u32[]{:S(2)}) async-start(bf16[4,192,1024]{2,1,0:T(8,128)(2,1)} %bitcast.156), calls=%async_computation.3 | async-start | bytes 3145728 | tf_op jit(solution)/shard_map/all_to_all | solution.py:115
  36.0 110.0 %all-gather.6.cloned.1.call-start = ((), (), s32[]{:S(2)}) async-start(), calls=%async_computation.5 | async-start | bytes 4718592 | tf_op jit(solution)/shard_map/all_gather | solution.py:146
  61.8 219.6 %all-gather.8.cloned.1.call-start = ((), (), s32[]{:S(2)}) async-start(), calls=%async_computation.6 | async-start | bytes 15728640 | tf_op jit(solution)/shard_map/all_gather | solution.py:62
  62.6 248.7 %all-gather.10.cloned.1.call-start = ((), (), s32[]{:S(2)}) async-start(), calls=%async_computation.7 | async-start | bytes 5242880 | tf_op jit(solution)/shard_map/all_gather | solution.py:63
  63.3 271.2 %all-gather.14.cloned.1.call-start = ((), (), s32[]{:S(2)}) async-start(), calls=%async_computation.11 | async-start | bytes 4718592 | tf_op jit(solution)/shard_map/all_gather | solution.py:147
  63.9 346.2 %all-gather.12.cloned.1.call-start = ((), (), s32[]{:S(2)}) async-start(), calls=%async_computation.9 | async-start | bytes 14417920 | tf_op jit(solution)/shard_map/all_gather | solution.py:70
  64.5 510.7 %all-reduce.10.cloned.1.call-start = ((), (), s32[]{:S(2)}) async-start(), calls=%async_computation.8 | async-start | bytes 12582912 | tf_op jit(solution)/shard_map/psum | solution.py:179
  64.5 79.5 %collective-permute-start.1 = (bf16[2,512,2816]{2,1,0:T(8,128)(2,1)}, bf16[2,512,2816]{2,1,0:T(8,128)(2,1)}, u32[]{:S(2)}, u32[]{:S(2)}) collective-permute-start(bf16[2,512,2816]{2,1,0:T(8,128)(2,1)} %param.32), channel_id=1, source_target_pairs={{0,8},{8,16},{16,24},{24,0},{1,9},{9,17},{17,25},{25,1},{2,10},{10... | collective-permute-start | bytes 17301512 | tf_op jit(solution)/shard_map/ppermute | solution.py:20
  144.0 137.3 %collective-permute-start.2 = (bf16[2,512,2816]{2,1,0:T(8,128)(2,1)}, bf16[2,512,2816]{2,1,0:T(8,128)(2,1)}, u32[]{:S(2)}, u32[]{:S(2)}) collective-permute-start(bf16[2,512,2816]{2,1,0:T(8,128)(2,1)} %collective-permute-done.1), channel_id=1, source_target_pairs={{0,8},{8,16},{16,24},{24,0},{1,9},{9,17},{17,25},{25,1},{2,10},{10... | collective-permute-start | bytes 17301512 | tf_op jit(solution)/shard_map/ppermute | solution.py:20
  144.2 430.9 %copy-start.66 = (s32[128]{0:T(128)}, s32[128]{0:T(128)S(1)}, u32[]{:S(2)}) copy-start(s32[128]{0:T(128)S(1)} %and_select_fusion) | copy-start | bytes 1540
  144.5 430.7 %copy-start.44 = (s32[768]{0:T(1024)}, s32[768]{0:T(1024)S(1)}, u32[]{:S(2)}) copy-start(s32[768]{0:T(1024)S(1)} %select_reduce_fusion) | copy-start | bytes 9220
  281.3 93.6 %collective-permute-start.3 = (bf16[2,512,2816]{2,1,0:T(8,128)(2,1)}, bf16[2,512,2816]{2,1,0:T(8,128)(2,1)}, u32[]{:S(2)}, u32[]{:S(2)}) collective-permute-start(bf16[2,512,2816]{2,1,0:T(8,128)(2,1)} %collective-permute-done.2), channel_id=1, source_target_pairs={{0,8},{8,16},{16,24},{24,0},{1,9},{9,17},{17,25},{25,1},{2,10},{10... | collective-permute-start | bytes 17301512 | tf_op jit(solution)/shard_map/ppermute | solution.py:20
  301.0 5.6 collective-permute-start
  305.4 274.5 %copy-start.50 = (f32[2048]{0:T(1024)}, f32[2048]{0:T(1024)S(1)}, u32[]{:S(2)}) copy-start(f32[2048]{0:T(1024)S(1)} %convert_element_type.143) | copy-start | bytes 24580
  319.3 517.4 %all-reduce.16.cloned.1.call-start = ((), (), s32[]{:S(2)}) async-start(), calls=%async_computation.14 | async-start | bytes 14155776 | tf_op jit(solution)/shard_map/psum | solution.py:241
  666.1 299.8 %reduce-scatter.2.cloned.1.call-start = ((), (), s32[]{:S(2)}) async-start(), calls=%async_computation.10 | async-start | bytes 4718592 | tf_op jit(solution)/shard_map/reduce_scatter | solution.py:201
  666.1 170.7 %copy-start.51 = (f32[2048]{0:T(1024)S(1)}, f32[2048]{0:T(1024)}, u32[]{:S(2)}) copy-start(f32[2048]{0:T(1024)} %copy-done.50) | copy-start | bytes 24580
  666.1 170.6 %copy-start.55 = (f32[768]{0:T(1024)S(1)}, f32[768]{0:T(1024)}, u32[]{:S(2)}) copy-start(f32[768]{0:T(1024)} %copy-done.54) | copy-start | bytes 9220
  680.6 156.2 %copy-start.33 = (bf16[2048,256]{1,0:T(8,128)(2,1)S(1)}, bf16[2048,256]{1,0:T(8,128)(2,1)}, u32[]{:S(2)}) copy-start(bf16[2048,256]{1,0:T(8,128)(2,1)} %param.38) | copy-start | bytes 3145732
  680.6 380.4 %all-reduce.12.cloned.1.call-start = ((), (), s32[]{:S(2)}) async-start(), calls=%async_computation.12 | async-start | bytes 12582912 | tf_op jit(solution)/shard_map/psum | solution.py:279
  865.6 5.5 collective-permute-start.4
  891.4 397.6 %all-reduce.14.cloned.1.call-start = ((), (), s32[]{:S(2)}) async-start(), calls=%async_computation.13 | async-start | bytes 23330816 | tf_op jit(solution)/shard_map/psum | solution.py:301
  1114.1 177.9 %all-to-all-start.3 = ((bf16[4,192,1024]{2,1,0:T(8,128)(2,1)}), bf16[4,192,1024]{2,1,0:T(8,128)(2,1)}, u32[]{:S(2)}, u32[]{:S(2)}) async-start(bf16[4,192,1024]{2,1,0:T(8,128)(2,1)} %get-tuple-element.66), calls=%async_computation.4 | async-start | bytes 3145728 | tf_op jit(solution)/shard_map/all_to_all | solution.py:295
  (80 other events, 2032.0 us)
Sparse Core Ops, SparseCore 0:
  61.9 46.0 all-gather.5
  109.6 114.2 all-gather.7
  225.4 45.7 all-gather.9
  273.2 44.9 all-gather.13
  319.6 90.4 all-gather.11
  412.4 162.7 all-reduce.9
  666.2 170.5 all-reduce.15
  839.0 43.3 reduce-scatter.1
  891.5 169.4 all-reduce.11
  1066.8 222.1 all-reduce.13
